TPU v7x, 32 devices: a whole 2x2x4 slice. The times are simulated.
32 devices in a mesh: scene: 2 (over y), tok: 4 (over z), col: 2 (over x), rep: 2 (over core).
Axes of the slice: x: 2, y: 2, z: 4, core: 2. Of those that a mesh axis runs over, the one named last changes fastest.
Arguments:
- tokens: float32 [8192, 512], P(('scene', 'tok'), ('col', 'rep')), parts along dimension 0
- w_qkv: float32 [2, 3, 512, 512], P(None, None, None, ('col', 'rep'))
- w_out: float32 [2, 512, 512], P(None, ('col', 'rep')), may hold values from -0.25 to 0.25
- w_up: float32 [2, 512, 2048], P(None, None, ('col', 'rep')), may hold values from -0.25 to 0.25
- w_down: float32 [2, 2048, 512], P(None, ('col', 'rep')), may hold values from -0.125 to 0.125
- attn_gain: float32 [2, 512], replicated, may hold values from 0.1 to 1.9
- mlp_gain: float32 [2, 512], replicated, may hold values from 0.1 to 1.9
- dest_device: int32 [128], P(('scene', 'tok')), parts along dimension 0, may hold values from 0 to 3, as said below
- dest_slot: int32 [128], P(('scene', 'tok')), parts along dimension 0, may hold values from 0 to 15, as said below
- pillar: int32 [8192], P(('scene', 'tok')), parts along dimension 0, may hold values from -1 to 2047, as said below
- depth_weight: float32 [2, 3, 3, 512], replicated, may hold values from -2 to 2
- point_weight: float32 [2, 512, 1024], replicated, may hold values from -0.25 to 0.25
- raster_gain: float32 [2, 512], replicated, may hold values from 0.1 to 1.9
Outputs:
- raster: float32 [128, 32, 512], P(('scene', 'tok', 'rep'), 'col'), parts along dimension 0
There are 2 independent parts, one for each index of `scene`. A program takes and returns all parts, laid end to end along the dimension named above; an argument that names none is the same for every part. Nothing has to cross between parts.
Inputs may be any that keep to these rules, and one draw needn't show every extreme that they name: `dest_device`: together with dest_slot the blocks fill every index of tok's 16 slots exactly once. At most 5 blocks of one index of tok go to one index, and every index sends exactly 5 blocks to some index. `dest_slot`: the slot of the block among the 16 of its destination. The token at Hilbert position t has a cell in raster rows i * 16 to (i + 1) * 16 - 1 with i = t // 1024, or -1 if it has no pillar; several tokens may share a cell.
All inputs are finite; a program needn't handle non-finite values.
Results may differ from a plain program's by a relative error of at most 0.00012.
Values sent between devices are 32-bit elements; how exact they have to be, the bound alone decides.
A program may use at most 128 MiB of HBM per device.

v0:
```python
import jax
import jax.numpy as jnp
from jax import lax
from jax.sharding import PartitionSpec as P

PATCH = 1024
TR = 16
TC = 16
HD = 16
MATMUL_PRECISION = lax.Precision.HIGHEST
EPSILON = 1e-05


def padded(block, sides, width):
    for axis, dim in sides:
        count = lax.axis_size(axis)
        forward = [(i, i + 1) for i in range(count - 1)]
        backward = [(target, source) for source, target in forward]
        low = lax.ppermute(
            lax.slice_in_dim(block, block.shape[dim] - width, None, axis=dim), axis, forward
        )
        high = lax.ppermute(lax.slice_in_dim(block, 0, width, axis=dim), axis, backward)
        block = jnp.concatenate([low, block, high], axis=dim)
    return block


def layer_norm(values, gain_row):
    average = jnp.mean(values, axis=-1, keepdims=True)
    centered = values - average
    variance = jnp.mean(centered * centered, axis=-1, keepdims=True)
    return centered * lax.rsqrt(variance + EPSILON) * gain_row


def patch_attention(query_projection, key_proj, value_proj):
    scores = jnp.einsum(
        "qhd,khd->hqk", query_projection, key_proj, precision=MATMUL_PRECISION
    ) * HD ** (-0.5)
    scores = scores - jnp.max(scores, axis=-1, keepdims=True)
    weights = jnp.exp(scores)
    weights = weights / jnp.sum(weights, axis=-1, keepdims=True)
    return jnp.einsum("hqk,khd->qhd", weights, value_proj, precision=MATMUL_PRECISION)


def matmul(left, right):
    return jnp.dot(left, right, precision=MATMUL_PRECISION, preferred_element_type=jnp.float32)


def widen(slice_cols):
    return lax.all_gather(slice_cols, ("col", "rep"), axis=1, tiled=True)


def block_layer(stream, layer_index, w_qkv, w_out, w_up, w_down, attn_gain, mlp_gain):
    row_count = stream.shape[0]
    local_cols = w_qkv.shape[-1]
    heads_here = local_cols // HD
    normed = layer_norm(stream, attn_gain[layer_index])
    shaped = tuple(
        (
            matmul(normed, w_qkv[layer_index, j]).reshape(row_count // PATCH, PATCH, heads_here, HD)
            for j in range(3)
        )
    )

    def attend_patch(operands):
        return patch_attention(operands[0], operands[1], operands[2]).reshape(PATCH, local_cols)

    attended = lax.map(attend_patch, shaped).reshape(row_count, local_cols)
    partial_out = matmul(attended, w_out[layer_index])
    stream = stream + lax.psum(partial_out, ("col", "rep"))
    normed = layer_norm(stream, mlp_gain[layer_index])
    hidden = jax.nn.gelu(matmul(normed, w_up[layer_index]), approximate=False)
    partial_mlp = matmul(hidden, w_down[layer_index])
    summed_share = lax.psum_scatter(partial_mlp, ("col", "rep"), scatter_dimension=1, tiled=True)
    feature_width = summed_share.shape[1]
    own_cols = lax.dynamic_slice_in_dim(
        stream, lax.axis_index(("col", "rep")) * feature_width, feature_width, 1
    )
    return own_cols + summed_share


def send_blocks(block_list, dest_device, dest_slot):
    block_count, rows_per_block, feature_width = block_list.shape
    peers = lax.axis_size("tok")
    capacity = max(2, (block_count + peers - 4) // (peers - 1))
    order_index = jnp.arange(block_count, dtype=jnp.int32)
    earlier = (dest_device[:, None] == dest_device[None, :]) & (
        order_index[None, :] < order_index[:, None]
    )
    prior_count = jnp.sum(earlier.astype(jnp.int32), axis=1)
    slot_key = dest_device * capacity + prior_count
    select_entries = (
        jnp.arange(peers * capacity, dtype=jnp.int32)[:, None] == slot_key[None, :]
    ).astype(jnp.float32)
    outgoing = jnp.einsum(
        "jb,brf->jrf", select_entries, block_list, precision=MATMUL_PRECISION
    ).reshape(peers, capacity, rows_per_block, feature_width)
    slot_codes = matmul(select_entries, (dest_slot + 1).astype(jnp.float32)).reshape(
        peers, capacity
    )
    incoming, arrived = (
        lax.all_to_all(outgoing, "tok", split_axis=0, concat_axis=0, tiled=True),
        lax.all_to_all(slot_codes, "tok", split_axis=0, concat_axis=0, tiled=True),
    )
    wanted = (order_index + 1).astype(jnp.float32)
    placing = (wanted[:, None] == arrived.reshape(-1)[None, :]).astype(jnp.float32)
    flat_incoming = incoming.reshape(peers * capacity, rows_per_block, feature_width)
    return jnp.einsum("sj,jrf->srf", placing, flat_incoming, precision=MATMUL_PRECISION)


def raster_cells(extended, depth_weight, point_weight, gain_row):
    row_count = extended.shape[0] - 2
    col_count = extended.shape[1] - 2
    count_of_channels = extended.shape[2]
    normed = (
        extended
        * lax.rsqrt(jnp.mean(extended * extended, axis=-1, keepdims=True) + EPSILON)
        * gain_row
    )
    mixed_cells = jnp.zeros((row_count, col_count, count_of_channels), jnp.float32)
    for row_tap in range(3):
        for col_tap in range(3):
            mixed_cells = (
                mixed_cells
                + normed[row_tap : row_tap + row_count, col_tap : col_tap + col_count]
                * depth_weight[row_tap, col_tap]
            )
    combined = matmul(mixed_cells.reshape(row_count * col_count, count_of_channels), point_weight)
    combined = combined.reshape(row_count, col_count, 2 * count_of_channels)
    centre = extended[1:-1, 1:-1]
    return centre + combined[..., :count_of_channels] * jax.nn.sigmoid(
        combined[..., count_of_channels:]
    )


def on_device(
    tokens,
    w_qkv,
    w_out,
    w_up,
    w_down,
    attn_gain,
    mlp_gain,
    dest_device,
    dest_slot,
    pillar,
    depth_weight,
    point_weight,
    raster_gain,
):
    stream = widen(tokens)
    first_out = block_layer(stream, 0, w_qkv, w_out, w_up, w_down, attn_gain, mlp_gain)
    feature_width = first_out.shape[1]
    block_count = dest_device.shape[0]
    block_list = first_out.reshape(block_count, first_out.shape[0] // block_count, feature_width)
    reordered_tokens = send_blocks(block_list, dest_device, dest_slot)
    stream = widen(reordered_tokens.reshape(-1, feature_width))
    stream = widen(block_layer(stream, 1, w_qkv, w_out, w_up, w_down, attn_gain, mlp_gain))
    rep_rows = TR // lax.axis_size("rep")
    row_start = lax.axis_index(("tok", "rep")) * rep_rows
    col_start = lax.axis_index("col") * TC
    full_width = TC * lax.axis_size("col")
    cell_rows = row_start + jnp.arange(rep_rows, dtype=jnp.int32)[:, None]
    cell_ids = (
        cell_rows * full_width + col_start + jnp.arange(TC, dtype=jnp.int32)[None, :]
    ).reshape(-1)
    onehot = (pillar[:, None] == cell_ids[None, :]).astype(jnp.float32)
    raster = jnp.einsum("tc,td->cd", onehot, stream, precision=MATMUL_PRECISION).reshape(
        rep_rows, TC, -1
    )
    for layer_index in range(2):
        extended = padded(raster, ((("tok", "rep"), 0), ("col", 1)), 1)
        raster = raster_cells(
            extended, depth_weight[layer_index], point_weight[layer_index], raster_gain[layer_index]
        )
    return raster


def solution(mesh):
    placed = (
        P(("scene", "tok"), ("col", "rep")),
        P(None, None, None, ("col", "rep")),
        P(None, ("col", "rep"), None),
        P(None, None, ("col", "rep")),
        P(None, ("col", "rep"), None),
        P(),
        P(),
        P(("scene", "tok")),
        P(("scene", "tok")),
        P(("scene", "tok")),
        P(),
        P(),
        P(),
    )
    return jax.shard_map(
        on_device,
        mesh=mesh,
        in_specs=placed,
        out_specs=P(("scene", "tok", "rep"), "col", None),
        check_vma=False,
    )
```

profile of v0, /device:TPU:1, one launch (start us, length us, event | category | flops | bytes accessed | tf_op | source)
XLA Modules:
  0.0 510.4 jit_solution(3229951573968464027)
XLA Ops:
  9.9 24.3 %all-gather.4.cloned.1.call-done = f32[1024,512]{1,0:T(8,128)} async-done(((f32[1024,128]{1,0:T(8,128)}), f32[1024,512]{1,0:T(8,128)}) %all-gather.4.cloned.1.call-update) | async-done | bytes 2097168 | tf_op jit(solution)/shard_map/all_gather | solution.py:49
  42.0 28.0 %multiply_reduce_fusion.1 = (f32[8,1024]{1,0:T(8,128)S(1)}, f32[8,1024,1024]{1,2,0:T(8,128)S(1)}) fusion(f32[1024,8,16]{0,2,1:T(8,128)S(1)} %fusion.32, f32[1024,8,16]{0,2,1:T(8,128)S(1)} %fusion.30), kind=kOutput, calls=%fused_computation.7 | convolution fusion | flops 1627381760 | bytes 34635776 | tf_op jit(solution)/shard_map/while/body/eval_jaxpr/qhd,khd->hqk/dot_general | solution.py:35
  70.0 5.9 %fusion.4 = f32[8,1024]{1,0:T(8,128)S(1)} fusion(f32[8,1024,1024]{1,2,0:T(8,128)S(1)} %get-tuple-element.80, f32[8,1024]{1,0:T(8,128)S(1)} %get-tuple-element.79), kind=kLoop, calls=%fused_computation.8 | loop fusion | flops 25157632 | bytes 33619968 | tf_op jit(solution)/shard_map/while/body/eval_jaxpr/reduce_sum | solution.py:40
  75.9 5.2 %copy-done = f32[8,1024,1024]{1,2,0:T(8,128)} copy-done((f32[8,1024,1024]{1,2,0:T(8,128)}, f32[8,1024,1024]{1,2,0:T(8,128)S(1)}, u32[]{:S(2)}) %copy-start) | copy-done | bytes 33554456
  81.1 3.4 fusion.34
  84.4 25.6 %fusion.2 = f32[8,16,1024]{2,1,0:T(8,128)S(1)} fusion(f32[1024,8,16]{0,2,1:T(8,128)} %fusion.34, f32[8,1024,1024]{1,2,0:T(8,128)} %copy-done, f32[8,1024]{1,0:T(8,128)S(1)} %fusion.4, f32[8,1024]{1,0:T(8,128)S(1)} %get-tuple-element.79), kind=kOutput, calls=%fused_computation.4 | convolution fusion | flops 1635778560 | bytes 34668544 | tf_op jit(solution)/shard_map/while/body/eval_jaxpr/hqk,khd->qhd/dot_general | solution.py:41
  110.0 4.1 fusion.299
  114.3 50.8 %all-reduce.3.cloned.1.call-done = f32[1024,512]{1,0:T(8,128)} async-done(((f32[1024,512]{1,0:T(8,128)}), f32[1024,512]{1,0:T(8,128)}) %all-reduce.3.cloned.1.call-update) | async-done | bytes 2097168 | tf_op jit(solution)/shard_map/psum | solution.py:69
  169.3 3.7 fusion.143
  173.0 9.5 %fusion.14 = f32[1024,512]{1,0:T(8,128)} fusion(f32[1024,512]{1,0:T(8,128)S(1)} %fusion.143, f32[2,512,512]{2,1,0:T(8,128)S(1)} %copy-done.15), kind=kOutput, calls=%fused_computation.20 | convolution fusion | flops 3254779904 | bytes 5242880 | tf_op jit(solution)/shard_map/dot_general | solution.py:45
  184.1 4.3 all-to-all-start
  188.5 25.5 %reduce-scatter.3.cloned.1.call-done = f32[1024,128]{1,0:T(8,128)} async-done(((f32[1024,512]{1,0:T(8,128)}), f32[1024,128]{1,0:T(8,128)}) %reduce-scatter.3.cloned.1.call-update) | async-done | bytes 524304 | tf_op jit(solution)/shard_map/reduce_scatter | solution.py:73
  217.1 4.3 all-to-all-start.1
  222.7 15.6 %all-to-all-done.1 = f32[4,5,64,128]{3,2,1,0:T(8,128)S(1)} async-done(((f32[4,5,64,128]{3,2,1,0:T(8,128)}), f32[4,5,64,128]{3,2,1,0:T(8,128)S(1)}, u32[]{:S(2)}, u32[]{:S(2)}) %all-to-all-start.1) | async-done | bytes 655392 | tf_op jit(solution)/shard_map/all_to_all | solution.py:101
  240.6 21.8 %all-gather.6.cloned.1.call-done = f32[1024,512]{1,0:T(8,128)} async-done(((f32[1024,128]{1,0:T(8,128)}), f32[1024,512]{1,0:T(8,128)}) %all-gather.6.cloned.1.call-update) | async-done | bytes 2097168 | tf_op jit(solution)/shard_map/all_gather | solution.py:49
  270.1 27.9 %multiply_reduce_fusion = (f32[8,1024]{1,0:T(8,128)S(1)}, f32[8,1024,1024]{1,2,0:T(8,128)S(1)}) fusion(f32[1024,8,16]{0,2,1:T(8,128)S(1)} %fusion.26, f32[1024,8,16]{0,2,1:T(8,128)S(1)} %fusion.24), kind=kOutput, calls=%fused_computation.6 | convolution fusion | flops 1627381760 | bytes 34635776 | tf_op jit(solution)/shard_map/while/body/eval_jaxpr/qhd,khd->hqk/dot_general | solution.py:35
  298.0 5.9 %fusion.5 = f32[8,1024]{1,0:T(8,128)S(1)} fusion(f32[8,1024,1024]{1,2,0:T(8,128)S(1)} %get-tuple-element.82, f32[8,1024]{1,0:T(8,128)S(1)} %get-tuple-element.81), kind=kLoop, calls=%fused_computation.9 | loop fusion | flops 25157632 | bytes 33619968 | tf_op jit(solution)/shard_map/while/body/eval_jaxpr/reduce_sum | solution.py:40
  303.9 5.2 %copy-done.1 = f32[8,1024,1024]{1,2,0:T(8,128)} copy-done((f32[8,1024,1024]{1,2,0:T(8,128)}, f32[8,1024,1024]{1,2,0:T(8,128)S(1)}, u32[]{:S(2)}) %copy-start.1) | copy-done | bytes 33554456
  311.7 25.0 %fusion = f32[8,16,1024]{2,1,0:T(8,128)S(1)} fusion(f32[1024,8,16]{0,2,1:T(8,128)S(1)} %fusion.28, f32[8,1024,1024]{1,2,0:T(8,128)} %copy-done.1, f32[8,1024]{1,0:T(8,128)S(1)} %fusion.5, f32[8,1024]{1,0:T(8,128)S(1)} %get-tuple-element.81), kind=kOutput, calls=%fused_computation.2 | convolution fusion | flops 1635778560 | bytes 34668544 | tf_op jit(solution)/shard_map/while/body/eval_jaxpr/hqk,khd->qhd/dot_general | solution.py:41
  336.7 4.1 fusion.297
  340.8 50.8 %all-reduce.5.cloned.1.call-done = f32[1024,512]{1,0:T(8,128)} async-done(((f32[1024,512]{1,0:T(8,128)}), f32[1024,512]{1,0:T(8,128)}) %all-reduce.5.cloned.1.call-update) | async-done | bytes 2097168 | tf_op jit(solution)/shard_map/psum | solution.py:69
  395.9 3.7 fusion.89
  399.6 9.5 %fusion.18 = f32[1024,512]{1,0:T(8,128)} fusion(f32[1024,512]{1,0:T(8,128)S(1)} %fusion.89, f32[2,512,512]{2,1,0:T(8,128)S(1)} %copy-done.16), kind=kOutput, calls=%fused_computation.23 | convolution fusion | flops 3254779904 | bytes 5242880 | tf_op jit(solution)/shard_map/dot_general | solution.py:45
  409.2 31.4 %reduce-scatter.5.cloned.1.call-done = f32[1024,128]{1,0:T(8,128)} async-done(((f32[1024,512]{1,0:T(8,128)}), f32[1024,128]{1,0:T(8,128)}) %reduce-scatter.5.cloned.1.call-update) | async-done | bytes 524304 | tf_op jit(solution)/shard_map/reduce_scatter | solution.py:73
  442.9 23.3 %all-gather.8.cloned.1.call-done = f32[1024,512]{1,0:T(8,128)} async-done(((f32[1024,128]{1,0:T(8,128)}), f32[1024,512]{1,0:T(8,128)}) %all-gather.8.cloned.1.call-update) | async-done | bytes 2097168 | tf_op jit(solution)/shard_map/all_gather | solution.py:49
  466.3 2.8 fusion.253
  469.1 3.3 collective-permute-start
  474.3 3.3 collective-permute-done.1
  481.1 3.2 collective-permute-done.3
  486.2 3.3 collective-permute-start.4
  491.5 3.3 collective-permute-done.5
  497.6 3.2 collective-permute-done.7
  (128 shorter events, 55.0 us)
Async XLA Ops:
  6.5 27.7 %all-gather.4.cloned.1.call-start = ((), (), s32[]{:S(2)}) async-start(), calls=%async_computation.4 | async-start | bytes 2621440 | tf_op jit(solution)/shard_map/all_gather | solution.py:49
  7.3 2.6 copy-start.10
  7.3 157.8 %all-reduce.3.cloned.1.call-start = ((), (), s32[]{:S(2)}) async-start(), calls=%async_computation.5 | async-start | bytes 4194304 | tf_op jit(solution)/shard_map/psum | solution.py:69
  36.4 3.0 copy-start.8
  70.0 11.1 %copy-start = (f32[8,1024,1024]{1,2,0:T(8,128)}, f32[8,1024,1024]{1,2,0:T(8,128)S(1)}, u32[]{:S(2)}) copy-start(f32[8,1024,1024]{1,2,0:T(8,128)S(1)} %get-tuple-element.80) | copy-start | bytes 100663296
  110.0 4.2 copy-start.11
  114.2 99.8 %reduce-scatter.3.cloned.1.call-start = ((), (), s32[]{:S(2)}) async-start(), calls=%async_computation.6 | async-start | bytes 2621440 | tf_op jit(solution)/shard_map/reduce_scatter | solution.py:73
  166.9 6.0 %copy-start.4 = (f32[1024,512]{1,0:T(8,128)}, f32[1024,512]{1,0:T(8,128)S(1)}, u32[]{:S(2)}) copy-start(f32[1024,512]{1,0:T(8,128)S(1)} %get-tuple-element.31) | copy-start | bytes 6291460
  167.0 2.4 copy-start.6
  169.3 3.7 copy-start.15
  184.1 33.0 %all-to-all-start = ((f32[4,1,5]{2,1,0:T(1,128)}), f32[4,1,5]{2,1,0:T(1,128)S(1)}, u32[]{:S(2)}, u32[]{:S(2)}) async-start(f32[4,1,5]{2,1,0:T(1,128)} %bitcast.2), calls=%async_computation | async-start | bytes 4096 | tf_op jit(solution)/shard_map/all_to_all | solution.py:102
  217.1 21.2 %all-to-all-start.1 = ((f32[4,5,64,128]{3,2,1,0:T(8,128)}), f32[4,5,64,128]{3,2,1,0:T(8,128)S(1)}, u32[]{:S(2)}, u32[]{:S(2)}) async-start(f32[4,5,64,128]{3,2,1,0:T(8,128)} %copy.48), calls=%async_computation.2 | async-start | bytes 1310720 | tf_op jit(solution)/shard_map/all_to_all | solution.py:101
  221.5 40.9 %all-gather.6.cloned.1.call-start = ((), (), s32[]{:S(2)}) async-start(), calls=%async_computation.7 | async-start | bytes 2621440 | tf_op jit(solution)/shard_map/all_gather | solution.py:49
  240.1 151.6 %all-reduce.5.cloned.1.call-start = ((), (), s32[]{:S(2)}) async-start(), calls=%async_computation.8 | async-start | bytes 4194304 | tf_op jit(solution)/shard_map/psum | solution.py:69
  298.0 11.1 %copy-start.1 = (f32[8,1024,1024]{1,2,0:T(8,128)}, f32[8,1024,1024]{1,2,0:T(8,128)S(1)}, u32[]{:S(2)}) copy-start(f32[8,1024,1024]{1,2,0:T(8,128)S(1)} %get-tuple-element.82) | copy-start | bytes 100663296
  340.8 99.8 %reduce-scatter.5.cloned.1.call-start = ((), (), s32[]{:S(2)}) async-start(), calls=%async_computation.9 | async-start | bytes 2621440 | tf_op jit(solution)/shard_map/reduce_scatter | solution.py:73
  393.6 6.0 %copy-start.5 = (f32[1024,512]{1,0:T(8,128)}, f32[1024,512]{1,0:T(8,128)S(1)}, u32[]{:S(2)}) copy-start(f32[1024,512]{1,0:T(8,128)S(1)} %get-tuple-element.24) | copy-start | bytes 6291460
  393.6 2.4 copy-start.7
  395.9 3.7 copy-start.16
  409.1 33.7 %copy-start.9 = (f32[2,3,3,512]{3,0,2,1:T(2,128)S(1)}, f32[2,3,3,512]{3,0,2,1:T(2,128)}, u32[]{:S(2)}) copy-start(f32[2,3,3,512]{3,0,2,1:T(2,128)} %param.23) | copy-start | bytes 110596
  409.1 57.1 %copy-start.13 = (s32[1024]{0:T(1024)S(1)}, s32[1024]{0:T(1024)}, u32[]{:S(2)}) copy-start(s32[1024]{0:T(1024)} %param.22) | copy-start | bytes 12292
  409.1 57.1 %all-gather.8.cloned.1.call-start = ((), (), s32[]{:S(2)}) async-start(), calls=%async_computation.10 | async-start | bytes 2621440 | tf_op jit(solution)/shard_map/all_gather | solution.py:49
  442.7 38.5 %copy-start.12 = (f32[2,512]{1,0:T(2,128)S(1)}, f32[2,512]{1,0:T(2,128)}, u32[]{:S(2)}) copy-start(f32[2,512]{1,0:T(2,128)} %param.25) | copy-start | bytes 12292
  466.3 18.4 %copy-start.14 = (f32[2,512,1024]{2,1,0:T(8,128)S(1)}, f32[2,512,1024]{2,1,0:T(8,128)}, u32[]{:S(2)}) copy-start(f32[2,512,1024]{2,1,0:T(8,128)} %param.24) | copy-start | bytes 12582916
  469.1 5.2 %collective-permute-start = (f32[1,16,512]{2,1,0:T(8,128)S(1)}, f32[1,16,512]{2,1,0:T(8,128)S(1)}, u32[]{:S(2)}, u32[]{:S(2)}) collective-permute-start(f32[1,16,512]{2,1,0:T(8,128)S(1)} %get-tuple-element.51), channel_id=1, source_target_pairs={{0,1},{1,4},{4,5},{5,8},{8,9},{9,12},{12,13},{2,3},{3,6},{6,7},{7,... | collective-permute-start | bytes 98312 | tf_op jit(solution)/shard_map/ppermute | solution.py:19
  472.4 5.2 %collective-permute-start.1 = (f32[1,16,512]{2,1,0:T(8,128)S(1)}, f32[1,16,512]{2,1,0:T(8,128)S(1)}, u32[]{:S(2)}, u32[]{:S(2)}) collective-permute-start(f32[1,16,512]{2,1,0:T(8,128)S(1)} %get-tuple-element.52), channel_id=1, source_target_pairs={{1,0},{4,1},{5,4},{8,5},{9,8},{12,9},{13,12},{3,2},{6,3},{7,6},{10... | collective-permute-start | bytes 98312 | tf_op jit(solution)/shard_map/ppermute | solution.py:22
  477.6 3.5 collective-permute-start.2
  479.8 4.5 collective-permute-start.3
  486.2 5.3 %collective-permute-start.4 = (f32[1,16,512]{2,1,0:T(8,128)S(1)}, f32[1,16,512]{2,1,0:T(8,128)S(1)}, u32[]{:S(2)}, u32[]{:S(2)}) collective-permute-start(f32[1,16,512]{2,1,0:T(8,128)S(1)} %get-tuple-element.49), channel_id=1, source_target_pairs={{0,1},{1,4},{4,5},{5,8},{8,9},{9,12},{12,13},{2,3},{3,6},{6,7},{7,... | collective-permute-start | bytes 98312 | tf_op jit(solution)/shard_map/ppermute | solution.py:19
  489.6 5.2 %collective-permute-start.5 = (f32[1,16,512]{2,1,0:T(8,128)S(1)}, f32[1,16,512]{2,1,0:T(8,128)S(1)}, u32[]{:S(2)}, u32[]{:S(2)}) collective-permute-start(f32[1,16,512]{2,1,0:T(8,128)S(1)} %get-tuple-element.50), channel_id=1, source_target_pairs={{1,0},{4,1},{5,4},{8,5},{9,8},{12,9},{13,12},{3,2},{6,3},{7,6},{10... | collective-permute-start | bytes 98312 | tf_op jit(solution)/shard_map/ppermute | solution.py:22
  494.9 2.7 collective-permute-start.6
  496.2 4.5 collective-permute-start.7
  (4 other events, 5.9 us)
Sparse Core Ops, SparseCore 0:
  8.9 25.2 all-gather.3
  114.3 50.7 all-reduce.2
  182.6 31.3 reduce-scatter.2
  240.2 22.0 all-gather.5
  340.9 50.7 all-reduce.4
  409.3 31.2 reduce-scatter.4
  442.8 23.4 all-gather.7
where the time goes:
time: 515 us; the launch traced here: 510 us
  waiting for transfers between devices  257 us (50%)
  matrix products  165 us (32%)
  other arithmetic  27 us (5%)
  starting transfers between devices  25.4 us (5%)
  local copies, waits for them, and re-layouts  21.6 us (4%)
  between operations  14.3 us (3%)
    psum x2, waiting for transfers between devices, block_layer(): stream = stream + lax.psum(partial_out, ('col', 'rep'))  102 us
    all_gather x3, waiting for transfers between devices, widen(): return lax.all_gather(slice_cols, ('col', 'rep'), axis=1, tiled=True)  69.4 us
    reduce_scatter x2, waiting for transfers between devices, block_layer(): lax.psum_scatter(partial_mlp, ('col', 'rep'), scatter_dimension=1, tiled=...  56.9 us
    dot_general x2, matrix products, patch_attention(): jnp.einsum('qhd,khd->hqk', query_projection, key_proj, precision=MATMUL_P...  56 us
    dot_general x15, matrix products, matmul(): jnp.dot(left, right, precision=MATMUL_PRECISION, preferred_element_type=j...  53.7 us
    dot_general x2, matrix products, patch_attention(): jnp.einsum('hqk,khd->qhd', weights, value_proj, precision=MATMUL_PRECISION)  50.6 us
    unnamed x45, local copies, waits for them, and re-layouts  16.8 us
    all_to_all x1, waiting for transfers between devices, send_blocks(): lax.all_to_all(outgoing, 'tok', split_axis=0, concat_axis=0, tiled=True)  15.6 us
  transfers between devices with their start and end apart: 17, of which 12 were waited for; matrix products, arithmetic and copies ran while one was open for 2% of the time, Pallas kernels for 0%

commit v1 on v0

--- a/solution.py
+++ b/solution.py
@@ -66,7 +66,7 @@
 
     attended = lax.map(attend_patch, shaped).reshape(row_count, local_cols)
     partial_out = matmul(attended, w_out[layer_index])
-    stream = stream + lax.psum(partial_out, ("col", "rep"))
+    stream = stream + lax.psum(lax.psum(partial_out, "rep"), "col")
     normed = layer_norm(stream, mlp_gain[layer_index])
     hidden = jax.nn.gelu(matmul(normed, w_up[layer_index]), approximate=False)
     partial_mlp = matmul(hidden, w_down[layer_index])

time: 515 us -> 588 us (1.14)
  waiting for transfers between devices: 257 us -> 330 us
    psum x2 -> x4, waiting for transfers between devices: 102 us -> 174 us  [block_layer(): stream = stream + lax.psum(lax.psum(partial_out, 'rep'), 'col')]
  transfers between devices with their start and end apart: 17 -> 19, of which waited for: 12 -> 14; matrix products, arithmetic and copies ran while one was open for 2% -> 1% of each run, Pallas kernels for 0% -> 0%
where the time goes in v1:
time: 588 us; the launch traced here: 583 us
  waiting for transfers between devices  330 us (56%)
  matrix products  165 us (28%)
  other arithmetic  27 us (5%)
  starting transfers between devices  25.5 us (4%)
  local copies, waits for them, and re-layouts  21.6 us (4%)
  between operations  14 us (2%)
    psum x4, waiting for transfers between devices, block_layer(): stream = stream + lax.psum(lax.psum(partial_out, 'rep'), 'col')  174 us
    all_gather x3, waiting for transfers between devices, widen(): return lax.all_gather(slice_cols, ('col', 'rep'), axis=1, tiled=True)  69.4 us
    reduce_scatter x2, waiting for transfers between devices, block_layer(): lax.psum_scatter(partial_mlp, ('col', 'rep'), scatter_dimension=1, tiled=...  56.7 us
    dot_general x2, matrix products, patch_attention(): jnp.einsum('qhd,khd->hqk', query_projection, key_proj, precision=MATMUL_P...  56 us
    dot_general x15, matrix products, matmul(): jnp.dot(left, right, precision=MATMUL_PRECISION, preferred_element_type=j...  53.7 us
    dot_general x2, matrix products, patch_attention(): jnp.einsum('hqk,khd->qhd', weights, value_proj, precision=MATMUL_PRECISION)  50.6 us
    unnamed x45, local copies, waits for them, and re-layouts  16.8 us
    all_to_all x1, waiting for transfers between devices, send_blocks(): lax.all_to_all(outgoing, 'tok', split_axis=0, concat_axis=0, tiled=True)  15.6 us
  transfers between devices with their start and end apart: 19, of which 14 were waited for; matrix products, arithmetic and copies ran while one was open for 1% of the time, Pallas kernels for 0%

profile of v1, /device:TPU:1, one launch (start us, length us, event | category | flops | bytes accessed | tf_op | source)
XLA Modules:
  0.0 582.8 jit_solution(1505125445887962174)
XLA Ops:
  9.9 24.3 %all-gather.4.cloned.1.call-done = f32[1024,512]{1,0:T(8,128)} async-done(((f32[1024,128]{1,0:T(8,128)}), f32[1024,512]{1,0:T(8,128)}) %all-gather.4.cloned.1.call-update) | async-done | bytes 2097168 | tf_op jit(solution)/shard_map/all_gather | solution.py:49
  42.0 28.0 %multiply_reduce_fusion.1 = (f32[8,1024]{1,0:T(8,128)S(1)}, f32[8,1024,1024]{1,2,0:T(8,128)S(1)}) fusion(f32[1024,8,16]{0,2,1:T(8,128)S(1)} %fusion.32, f32[1024,8,16]{0,2,1:T(8,128)S(1)} %fusion.30), kind=kOutput, calls=%fused_computation.7 | convolution fusion | flops 1627381760 | bytes 34635776 | tf_op jit(solution)/shard_map/while/body/eval_jaxpr/qhd,khd->hqk/dot_general | solution.py:35
  70.0 5.9 %fusion.4 = f32[8,1024]{1,0:T(8,128)S(1)} fusion(f32[8,1024,1024]{1,2,0:T(8,128)S(1)} %get-tuple-element.80, f32[8,1024]{1,0:T(8,128)S(1)} %get-tuple-element.79), kind=kLoop, calls=%fused_computation.8 | loop fusion | flops 25157632 | bytes 33619968 | tf_op jit(solution)/shard_map/while/body/eval_jaxpr/reduce_sum | solution.py:40
  75.9 5.2 copy-done
  81.1 3.4 fusion.34
  84.4 25.6 %fusion.2 = f32[8,16,1024]{2,1,0:T(8,128)S(1)} fusion(f32[1024,8,16]{0,2,1:T(8,128)} %fusion.34, f32[8,1024,1024]{1,2,0:T(8,128)} %copy-done, f32[8,1024]{1,0:T(8,128)S(1)} %fusion.4, f32[8,1024]{1,0:T(8,128)S(1)} %get-tuple-element.79), kind=kOutput, calls=%fused_computation.4 | convolution fusion | flops 1635778560 | bytes 34668544 | tf_op jit(solution)/shard_map/while/body/eval_jaxpr/hqk,khd->qhd/dot_general | solution.py:41
  110.0 4.1 fusion.299
  114.2 21.4 %all-reduce.5.cloned.1.call-done = f32[1024,512]{1,0:T(8,128)} async-done(((f32[1024,512]{1,0:T(8,128)}), f32[1024,512]{1,0:T(8,128)}) %all-reduce.5.cloned.1.call-update) | async-done | bytes 2097168 | tf_op jit(solution)/shard_map/psum | solution.py:69
  135.7 65.8 %all-reduce.7.cloned.1.call-done = f32[1024,512]{1,0:T(8,128)} async-done(((f32[1024,512]{1,0:T(8,128)}), f32[1024,512]{1,0:T(8,128)}) %all-reduce.7.cloned.1.call-update) | async-done | bytes 2097168 | tf_op jit(solution)/shard_map/psum | solution.py:69
  205.8 3.7 fusion.143
  209.5 9.5 %fusion.14 = f32[1024,512]{1,0:T(8,128)} fusion(f32[1024,512]{1,0:T(8,128)S(1)} %fusion.143, f32[2,512,512]{2,1,0:T(8,128)S(1)} %copy-done.15), kind=kOutput, calls=%fused_computation.20 | convolution fusion | flops 3254779904 | bytes 5242880 | tf_op jit(solution)/shard_map/dot_general | solution.py:45
  220.6 4.3 all-to-all-start
  224.9 25.4 %reduce-scatter.3.cloned.1.call-done = f32[1024,128]{1,0:T(8,128)} async-done(((f32[1024,512]{1,0:T(8,128)}), f32[1024,128]{1,0:T(8,128)}) %reduce-scatter.3.cloned.1.call-update) | async-done | bytes 524304 | tf_op jit(solution)/shard_map/reduce_scatter | solution.py:73
  253.5 4.3 all-to-all-start.1
  259.1 15.6 %all-to-all-done.1 = f32[4,5,64,128]{3,2,1,0:T(8,128)S(1)} async-done(((f32[4,5,64,128]{3,2,1,0:T(8,128)}), f32[4,5,64,128]{3,2,1,0:T(8,128)S(1)}, u32[]{:S(2)}, u32[]{:S(2)}) %all-to-all-start.1) | async-done | bytes 655392 | tf_op jit(solution)/shard_map/all_to_all | solution.py:101
  276.9 21.8 %all-gather.6.cloned.1.call-done = f32[1024,512]{1,0:T(8,128)} async-done(((f32[1024,128]{1,0:T(8,128)}), f32[1024,512]{1,0:T(8,128)}) %all-gather.6.cloned.1.call-update) | async-done | bytes 2097168 | tf_op jit(solution)/shard_map/all_gather | solution.py:49
  306.4 27.9 %multiply_reduce_fusion = (f32[8,1024]{1,0:T(8,128)S(1)}, f32[8,1024,1024]{1,2,0:T(8,128)S(1)}) fusion(f32[1024,8,16]{0,2,1:T(8,128)S(1)} %fusion.26, f32[1024,8,16]{0,2,1:T(8,128)S(1)} %fusion.24), kind=kOutput, calls=%fused_computation.6 | convolution fusion | flops 1627381760 | bytes 34635776 | tf_op jit(solution)/shard_map/while/body/eval_jaxpr/qhd,khd->hqk/dot_general | solution.py:35
  334.4 5.9 %fusion.5 = f32[8,1024]{1,0:T(8,128)S(1)} fusion(f32[8,1024,1024]{1,2,0:T(8,128)S(1)} %get-tuple-element.82, f32[8,1024]{1,0:T(8,128)S(1)} %get-tuple-element.81), kind=kLoop, calls=%fused_computation.9 | loop fusion | flops 25157632 | bytes 33619968 | tf_op jit(solution)/shard_map/while/body/eval_jaxpr/reduce_sum | solution.py:40
  340.3 5.2 copy-done.1
  348.0 25.0 %fusion = f32[8,16,1024]{2,1,0:T(8,128)S(1)} fusion(f32[1024,8,16]{0,2,1:T(8,128)S(1)} %fusion.28, f32[8,1024,1024]{1,2,0:T(8,128)} %copy-done.1, f32[8,1024]{1,0:T(8,128)S(1)} %fusion.5, f32[8,1024]{1,0:T(8,128)S(1)} %get-tuple-element.81), kind=kOutput, calls=%fused_computation.2 | convolution fusion | flops 1635778560 | bytes 34668544 | tf_op jit(solution)/shard_map/while/body/eval_jaxpr/hqk,khd->qhd/dot_general | solution.py:41
  373.0 4.1 fusion.297
  377.2 21.4 %all-reduce.9.cloned.1.call-done = f32[1024,512]{1,0:T(8,128)} async-done(((f32[1024,512]{1,0:T(8,128)}), f32[1024,512]{1,0:T(8,128)}) %all-reduce.9.cloned.1.call-update) | async-done | bytes 2097168 | tf_op jit(solution)/shard_map/psum | solution.py:69
  398.6 65.8 %all-reduce.11.cloned.1.call-done = f32[1024,512]{1,0:T(8,128)} async-done(((f32[1024,512]{1,0:T(8,128)}), f32[1024,512]{1,0:T(8,128)}) %all-reduce.11.cloned.1.call-update) | async-done | bytes 2097168 | tf_op jit(solution)/shard_map/psum | solution.py:69
  468.7 3.7 fusion.89
  472.4 9.5 %fusion.18 = f32[1024,512]{1,0:T(8,128)} fusion(f32[1024,512]{1,0:T(8,128)S(1)} %fusion.89, f32[2,512,512]{2,1,0:T(8,128)S(1)} %copy-done.16), kind=kOutput, calls=%fused_computation.23 | convolution fusion | flops 3254779904 | bytes 5242880 | tf_op jit(solution)/shard_map/dot_general | solution.py:45
  482.0 31.3 %reduce-scatter.5.cloned.1.call-done = f32[1024,128]{1,0:T(8,128)} async-done(((f32[1024,512]{1,0:T(8,128)}), f32[1024,128]{1,0:T(8,128)}) %reduce-scatter.5.cloned.1.call-update) | async-done | bytes 524304 | tf_op jit(solution)/shard_map/reduce_scatter | solution.py:73
  515.6 23.3 %all-gather.8.cloned.1.call-done = f32[1024,512]{1,0:T(8,128)} async-done(((f32[1024,128]{1,0:T(8,128)}), f32[1024,512]{1,0:T(8,128)}) %all-gather.8.cloned.1.call-update) | async-done | bytes 2097168 | tf_op jit(solution)/shard_map/all_gather | solution.py:49
  541.7 3.3 collective-permute-start
  547.0 3.3 collective-permute-done.1
  553.8 3.2 collective-permute-done.3
  558.9 3.3 collective-permute-start.4
  564.2 3.3 collective-permute-done.5
  (134 shorter events, 61.1 us)
Async XLA Ops:
  6.5 27.7 %all-gather.4.cloned.1.call-start = ((), (), s32[]{:S(2)}) async-start(), calls=%async_computation.4 | async-start | bytes 2621440 | tf_op jit(solution)/shard_map/all_gather | solution.py:49
  7.3 2.6 copy-start.10
  7.3 128.3 %all-reduce.5.cloned.1.call-start = ((), (), s32[]{:S(2)}) async-start(), calls=%async_computation.5 | async-start | bytes 4194304 | tf_op jit(solution)/shard_map/psum | solution.py:69
  36.4 3.0 copy-start.8
  70.0 11.1 %copy-start = (f32[8,1024,1024]{1,2,0:T(8,128)}, f32[8,1024,1024]{1,2,0:T(8,128)S(1)}, u32[]{:S(2)}) copy-start(f32[8,1024,1024]{1,2,0:T(8,128)S(1)} %get-tuple-element.80) | copy-start | bytes 100663296
  114.1 21.5 %copy-start.11 = (f32[2,512]{1,0:T(2,128)S(1)}, f32[2,512]{1,0:T(2,128)}, u32[]{:S(2)}) copy-start(f32[2,512]{1,0:T(2,128)} %param.19) | copy-start | bytes 12292
  114.2 87.4 %all-reduce.7.cloned.1.call-start = ((), (), s32[]{:S(2)}) async-start(), calls=%async_computation.6 | async-start | bytes 4194304 | tf_op jit(solution)/shard_map/psum | solution.py:69
  135.6 114.7 %reduce-scatter.3.cloned.1.call-start = ((), (), s32[]{:S(2)}) async-start(), calls=%async_computation.7 | async-start | bytes 2621440 | tf_op jit(solution)/shard_map/reduce_scatter | solution.py:73
  203.4 6.0 %copy-start.4 = (f32[1024,512]{1,0:T(8,128)}, f32[1024,512]{1,0:T(8,128)S(1)}, u32[]{:S(2)}) copy-start(f32[1024,512]{1,0:T(8,128)S(1)} %get-tuple-element.31) | copy-start | bytes 6291460
  205.8 3.7 copy-start.15
  220.6 32.8 %all-to-all-start = ((f32[4,1,5]{2,1,0:T(1,128)}), f32[4,1,5]{2,1,0:T(1,128)S(1)}, u32[]{:S(2)}, u32[]{:S(2)}) async-start(f32[4,1,5]{2,1,0:T(1,128)} %bitcast.2), calls=%async_computation | async-start | bytes 4096 | tf_op jit(solution)/shard_map/all_to_all | solution.py:102
  253.5 21.2 %all-to-all-start.1 = ((f32[4,5,64,128]{3,2,1,0:T(8,128)}), f32[4,5,64,128]{3,2,1,0:T(8,128)S(1)}, u32[]{:S(2)}, u32[]{:S(2)}) async-start(f32[4,5,64,128]{3,2,1,0:T(8,128)} %copy.48), calls=%async_computation.2 | async-start | bytes 1310720 | tf_op jit(solution)/shard_map/all_to_all | solution.py:101
  257.8 40.9 %all-gather.6.cloned.1.call-start = ((), (), s32[]{:S(2)}) async-start(), calls=%async_computation.8 | async-start | bytes 2621440 | tf_op jit(solution)/shard_map/all_gather | solution.py:49
  276.4 122.1 %all-reduce.9.cloned.1.call-start = ((), (), s32[]{:S(2)}) async-start(), calls=%async_computation.9 | async-start | bytes 4194304 | tf_op jit(solution)/shard_map/psum | solution.py:69
  334.4 11.1 %copy-start.1 = (f32[8,1024,1024]{1,2,0:T(8,128)}, f32[8,1024,1024]{1,2,0:T(8,128)S(1)}, u32[]{:S(2)}) copy-start(f32[8,1024,1024]{1,2,0:T(8,128)S(1)} %get-tuple-element.82) | copy-start | bytes 100663296
  377.1 87.3 %all-reduce.11.cloned.1.call-start = ((), (), s32[]{:S(2)}) async-start(), calls=%async_computation.10 | async-start | bytes 4194304 | tf_op jit(solution)/shard_map/psum | solution.py:69
  398.6 114.7 %reduce-scatter.5.cloned.1.call-start = ((), (), s32[]{:S(2)}) async-start(), calls=%async_computation.11 | async-start | bytes 2621440 | tf_op jit(solution)/shard_map/reduce_scatter | solution.py:73
  466.3 6.0 %copy-start.5 = (f32[1024,512]{1,0:T(8,128)}, f32[1024,512]{1,0:T(8,128)S(1)}, u32[]{:S(2)}) copy-start(f32[1024,512]{1,0:T(8,128)S(1)} %get-tuple-element.24) | copy-start | bytes 6291460
  468.7 3.7 copy-start.16
  481.9 33.6 %copy-start.9 = (f32[2,3,3,512]{3,0,2,1:T(2,128)S(1)}, f32[2,3,3,512]{3,0,2,1:T(2,128)}, u32[]{:S(2)}) copy-start(f32[2,3,3,512]{3,0,2,1:T(2,128)} %param.23) | copy-start | bytes 110596
  481.9 57.0 %copy-start.13 = (s32[1024]{0:T(1024)S(1)}, s32[1024]{0:T(1024)}, u32[]{:S(2)}) copy-start(s32[1024]{0:T(1024)} %param.22) | copy-start | bytes 12292
  481.9 57.0 %all-gather.8.cloned.1.call-start = ((), (), s32[]{:S(2)}) async-start(), calls=%async_computation.12 | async-start | bytes 2621440 | tf_op jit(solution)/shard_map/all_gather | solution.py:49
  515.3 38.4 %copy-start.12 = (f32[2,512]{1,0:T(2,128)S(1)}, f32[2,512]{1,0:T(2,128)}, u32[]{:S(2)}) copy-start(f32[2,512]{1,0:T(2,128)} %param.25) | copy-start | bytes 12292
  538.9 18.4 %copy-start.14 = (f32[2,512,1024]{2,1,0:T(8,128)S(1)}, f32[2,512,1024]{2,1,0:T(8,128)}, u32[]{:S(2)}) copy-start(f32[2,512,1024]{2,1,0:T(8,128)} %param.24) | copy-start | bytes 12582916
  541.7 5.2 collective-permute-start
  545.0 5.2 collective-permute-start.1
  550.3 3.5 collective-permute-start.2
  552.5 4.5 collective-permute-start.3
  558.9 5.3 collective-permute-start.4
  562.2 5.2 collective-permute-start.5
  567.5 2.7 collective-permute-start.6
  568.9 4.5 collective-permute-start.7
  (6 other events, 10.6 us)
Sparse Core Ops, SparseCore 0:
  8.9 25.2 all-gather.3
  114.3 21.2 all-reduce.4
  137.9 63.5 all-reduce.6
  219.1 31.1 reduce-scatter.2
  276.5 22.0 all-gather.5
  377.2 21.2 all-reduce.8
  400.8 63.5 all-reduce.10
  482.0 31.1 reduce-scatter.4
  515.5 23.3 all-gather.7
